TPU v7x, 32 devices: a whole 2x2x4 slice. The times are simulated.
32 devices in a mesh: lat: 8 (over y, x, core), lon: 4 (over z).
Axes of the slice: x: 2, y: 2, z: 4, core: 2. Of those that a mesh axis runs over, the one named last changes fastest.
Arguments:
- adjoint: float32 [8, 8, 256, 512], P(None, None, 'lat', 'lon'), may hold values from -6 to 6
- transport: float32 [6, 8, 256, 512], P(None, None, 'lat', 'lon'), may hold values from 0.03 to 0.14
- cell_weight: float32 [256, 512], P('lat', 'lon'), may hold values from 0.1 to 1
- region_local: int32 [256, 512], P('lat', 'lon'), may hold values from 0 to 255
- tile_regions: int32 [32, 256], replicated, may hold values from 0 to 2047, as said below
- polar_rows: int32 [256], P('lat'), may hold values 0 or 1
- week_index: int32 [1], replicated, may hold values from 0 to 51
- grad_in: bfloat16 [2048, 416], P(('lat', 'lon')), may hold values from -6 to 6
- covariance: bfloat16 [2048, 2048], P(('lat', 'lon')), may hold values from -0.25 to 0.25
Outputs:
- adjoint_out: float32 [8, 8, 256, 512], P(None, None, 'lat', 'lon')
- precond: float32 [2048, 416], P(('lat', 'lon'))
Inputs may be any that keep to these rules, and one draw needn't show every extreme that they name: `tile_regions`: each row holds 256 different region numbers; with per = 8, entries o * per to o * per + per - 1 of a row lie in regions o * 64 to o * 64 + 63, for every o.
All inputs are finite; a program needn't handle non-finite values. No bound on the sum of `polar_rows` on one device may be relied on, other than what follows from the above.
Results may differ from a plain program's by a relative error of at most 0.00066.
Values may be sent and summed in bfloat16 or wider, within the bound.
No kernel may reach another device: no remote copies, remote signals or barrier semaphores. Data moves between devices by JAX's collectives and lax.ppermute only.
A program may use at most 128 MiB of HBM per device.

v0:
```python
import jax
import jax.numpy as jnp
from jax import lax
from jax.sharding import PartitionSpec as P


def extended(x, sides, width):
    for axis, dim in sides:
        size, length = (lax.axis_size(axis), x.shape[dim])
        up = [(i, (i + 1) % size) for i in range(size)]
        down = [(j, i) for i, j in up]
        last = lax.slice_in_dim(x, length - width, length, axis=dim)
        leading = lax.slice_in_dim(x, 0, width, axis=dim)
        before = lax.ppermute(last, axis, up)
        after = lax.ppermute(leading, axis, down)
        x = jnp.concatenate([before, x, after], axis=dim)
    return x


def advance(padded, rates):
    centre = padded[:, :, 1:-1, 1:-1]
    to_east = padded[:, :, 1:-1, 2:] - centre
    to_west = padded[:, :, 1:-1, :-2] - centre
    to_north = padded[:, :, 2:, 1:-1] - centre
    to_south = padded[:, :, :-2, 1:-1] - centre
    flat_zero = jnp.zeros_like(centre[:, :1])
    upper = jnp.concatenate([centre[:, 1:] - centre[:, :-1], flat_zero], axis=1)
    lower = jnp.concatenate([flat_zero, centre[:, :-1] - centre[:, 1:]], axis=1)
    return (
        centre
        + rates[0] * to_east
        + rates[1] * to_west
        + rates[2] * to_north
        + rates[3] * to_south
        + rates[4] * upper
        + rates[5] * lower
    )


def pole_mask(padded, margin, interior):
    band = lax.axis_index("lat")
    last_band = lax.axis_size("lat") - 1
    row_ids = jnp.arange(interior + 2 * margin, dtype=jnp.int32)
    outside = (row_ids < margin) & (band == 0) | (row_ids >= interior + margin) & (
        band == last_band
    )
    return jnp.where(outside[None, None, :, None], 0.0, padded)


def shards(
    adjoint,
    transport,
    cell_weight,
    region_local,
    tile_regions,
    polar_rows,
    week_index,
    grad_in,
    covariance,
):
    tracers, levels, lat_rows, lon_cols = adjoint.shape
    region_count = covariance.shape[1]
    own_rows = covariance.shape[0]
    week_cols = grad_in.shape[1] // tracers
    lon_count = lax.axis_size("lon")
    my_tile = lax.axis_index("lat") * lon_count + lax.axis_index("lon")
    base = jnp.dot(
        covariance,
        lax.all_gather(grad_in, ("lat", "lon"), axis=0, tiled=True),
        preferred_element_type=jnp.float32,
    )
    field = adjoint
    for repeat in range(2):
        padded = extended(field, (("lat", 2), ("lon", 3)), 1)
        field = advance(pole_mask(padded, 1, lat_rows), transport)
    row_sums = lax.psum(jnp.sum(field, axis=3), "lon")
    zonal = row_sums / (lon_cols * lon_count)
    flags = polar_rows.astype(jnp.float32)[None, None, :, None]
    adjoint_out = field + 0.5 * flags * (zonal[..., None] - field)
    surface = (adjoint_out[:, 0] * cell_weight[None]).reshape(tracers, -1)
    local_count = tile_regions.shape[1]
    one_hot = (
        region_local.reshape(1, -1) == jnp.arange(local_count, dtype=jnp.int32)[:, None]
    ).astype(jnp.float32)
    local_sums = lax.dot_general(
        one_hot,
        surface,
        (((1,), (1,)), ((), ())),
        precision=lax.Precision.HIGHEST,
        preferred_element_type=jnp.float32,
    )
    my_regions = lax.dynamic_index_in_dim(tile_regions, my_tile, 0, keepdims=False)
    dense = jnp.zeros((region_count, tracers), jnp.float32).at[my_regions].add(local_sums)
    fresh_all = lax.psum(dense, ("lat", "lon")).astype(jnp.bfloat16)
    added = jnp.dot(covariance, fresh_all, preferred_element_type=jnp.float32)
    week_hot = (jnp.arange(week_cols, dtype=jnp.int32) == week_index[0]).astype(jnp.float32)
    precond = (
        base.reshape(own_rows, week_cols, tracers) + week_hot[None, :, None] * added[:, None, :]
    )
    return (adjoint_out, precond.reshape(own_rows, week_cols * tracers))


def solution(mesh):
    in_specs = (
        P(None, None, "lat", "lon"),
        P(None, None, "lat", "lon"),
        P("lat", "lon"),
        P("lat", "lon"),
        P(),
        P("lat"),
        P(),
        P(("lat", "lon"), None),
        P(("lat", "lon"), None),
    )
    out_specs = (P(None, None, "lat", "lon"), P(("lat", "lon"), None))
    return jax.shard_map(shards, mesh=mesh, in_specs=in_specs, out_specs=out_specs, check_vma=False)
```

profile of v0, /device:TPU:0, one launch (start us, length us, event | category | flops | bytes accessed | tf_op | source)
XLA Modules:
  0.0 179.2 jit_solution(4061105329152444854)
XLA Ops:
  8.9 2.9 %collective-permute-start.1 = (f32[8,8,1,128]{3,1,2,0:T(8,128)S(1)}, f32[8,8,1,128]{3,1,2,0:T(8,128)S(1)}, u32[]{:S(2)}, u32[]{:S(2)}) collective-permute-start(f32[8,8,1,128]{3,1,2,0:T(8,128)S(1)} %bitcast.36), channel_id=1, source_target_pairs={{4,0},{8,4},{12,8},{16,12},{20,16},{24,20},{28,24},{0,28},{5,1},{9... | collective-permute-start | bytes 98312 | tf_op jit(solution)/shard_map/ppermute | solution.py:15
  13.8 3.6 %copy.81 = f32[8,8,32,128]{2,1,3,0:T(8,128)} copy(f32[8,8,32,128]{3,2,1,0:T(8,128)} %param.9) | data formatting | bytes 2097152 | tf_op args[0]
  17.4 2.6 %copy.80 = f32[8,8,1,128]{2,1,3,0:T(8,128)} copy(f32[8,8,1,128]{3,1,2,0:T(8,128)S(1)} %collective-permute-done) | data formatting | bytes 65536 | tf_op jit(solution)/shard_map/ppermute | solution.py:14
  20.1 2.6 %copy.82 = f32[8,8,1,128]{2,1,3,0:T(8,128)} copy(f32[8,8,1,128]{3,1,2,0:T(8,128)S(1)} %collective-permute-done.1) | data formatting | bytes 65536 | tf_op jit(solution)/shard_map/ppermute | solution.py:15
  23.6 2.3 %collective-permute-start.2 = (f32[8,8,34,1]{2,1,3,0:T(8,128)S(1)}, f32[8,8,34,1]{2,1,3,0:T(8,128)S(1)}, u32[]{:S(2)}, u32[]{:S(2)}) collective-permute-start(f32[8,8,34,1]{2,1,3,0:T(8,128)S(1)} %get-tuple-element.16), channel_id=1, source_target_pairs={{0,1},{1,2},{2,3},{3,0},{4,5},{5,6},{6,7},{7,4},{8,9},{9,10},{10,1... | collective-permute-start | bytes 26120 | tf_op jit(solution)/shard_map/ppermute | solution.py:14
  26.0 2.1 %collective-permute-start.3 = (f32[8,8,34,1]{2,1,3,0:T(8,128)S(1)}, f32[8,8,34,1]{2,1,3,0:T(8,128)S(1)}, u32[]{:S(2)}, u32[]{:S(2)}) collective-permute-start(f32[8,8,34,1]{2,1,3,0:T(8,128)S(1)} %get-tuple-element.17), channel_id=1, source_target_pairs={{1,0},{2,1},{3,2},{0,3},{5,4},{6,5},{7,6},{4,7},{9,8},{10,9},{11,1... | collective-permute-start | bytes 26120 | tf_op jit(solution)/shard_map/ppermute | solution.py:15
  33.4 5.8 %maximum_select_fusion = f32[8,8,34,130]{2,1,3,0:T(8,128)S(1)} fusion(f32[8,8,34,1]{2,1,3,0:T(8,128)S(1)} %collective-permute-done.3, f32[8,8,1,128]{2,1,3,0:T(8,128)} %copy.82, f32[8,8,32,128]{2,1,3,0:T(8,128)} %copy.81, f32[8,8,1,128]{2,1,3,0:T(8,128)} %copy.80, f32[8,8,34,1]{2,1,3,0:T(8,128)S(1)} %collective-permute-done.2, pred[34]{0:T(512)(128)(4,1)S(1)} %and_or_fusion), kind=kLoop, calls=%fused_computation.1 | loop fusion | flops 1414400 | bytes 2263074 | tf_op jit(solution)/shard_map/jit(_where)/select_n | solution.py:47
  39.2 2.2 %slice_subtract_fusion.11 = (f32[8,7,32,128]{2,1,3,0:T(8,128)S(1)}, f32[8,7,32,128]{2,1,3,0:T(8,128)S(1)}) fusion(f32[8,8,34,130]{2,1,3,0:T(8,128)S(1)} %maximum_select_fusion), kind=kLoop, calls=%fused_computation.37 | loop fusion | flops 458752 | bytes 3670016 | tf_op jit(solution)/shard_map/sub | solution.py:27
  41.4 6.1 %fusion.13 = f32[8,8,32,128]{2,1,3,0:T(8,128)S(1)} fusion(f32[8,8,34,130]{2,1,3,0:T(8,128)S(1)} %maximum_select_fusion, f32[8,7,32,128]{2,1,3,0:T(8,128)S(1)} %get-tuple-element.21, f32[8,7,32,128]{2,1,3,0:T(8,128)S(1)} %get-tuple-element.20, f32[8,32,128]{1,0,2:T(8,128)} %copy.88, f32[8,32,128]{1,0,2:T(8,128)} %copy.87, f32[8,32,128]{1,0,2:T(8,128)} %copy.86, ...), kind=kLoop, calls=%fused_computation.21 | loop fusion | flops 4194304 | bytes 8912896 | tf_op jit(solution)/shard_map/add | solution.py:30
  47.6 4.6 %fusion.29 = (f32[8,8,1,128]{2,1,3,0:T(8,128)}, f32[8,8,1,128]{2,1,3,0:T(8,128)}) fusion(f32[8,8,32,128]{2,1,3,0:T(8,128)S(1)} %fusion.13), kind=kLoop, calls=%fused_computation.66 | loop fusion | bytes 131072 | tf_op jit(solution)/shard_map/slice | solution.py:12
  52.2 2.8 %copy.89 = f32[8,8,1,128]{3,1,2,0:T(8,128)S(1)} copy(f32[8,8,1,128]{2,1,3,0:T(8,128)} %get-tuple-element.22) | data formatting | bytes 65536 | tf_op jit(solution)/shard_map/slice | solution.py:12
  55.1 2.9 %copy.90 = f32[8,8,1,128]{3,1,2,0:T(8,128)S(1)} copy(f32[8,8,1,128]{2,1,3,0:T(8,128)} %get-tuple-element.23) | data formatting | bytes 65536 | tf_op jit(solution)/shard_map/slice | solution.py:13
  58.0 2.9 %collective-permute-start.5 = (f32[8,8,1,128]{3,1,2,0:T(8,128)S(1)}, f32[8,8,1,128]{3,1,2,0:T(8,128)S(1)}, u32[]{:S(2)}, u32[]{:S(2)}) collective-permute-start(f32[8,8,1,128]{3,1,2,0:T(8,128)S(1)} %copy.90), channel_id=1, source_target_pairs={{4,0},{8,4},{12,8},{16,12},{20,16},{24,20},{28,24},{0,28},{5,1},{9... | collective-permute-start | bytes 98312 | tf_op jit(solution)/shard_map/ppermute | solution.py:15
  62.2 2.7 %copy.91 = f32[8,8,1,128]{2,1,3,0:T(8,128)} copy(f32[8,8,1,128]{3,1,2,0:T(8,128)S(1)} %collective-permute-done.4) | data formatting | bytes 65536 | tf_op jit(solution)/shard_map/ppermute | solution.py:14
  64.9 2.7 %copy.92 = f32[8,8,1,128]{2,1,3,0:T(8,128)} copy(f32[8,8,1,128]{3,1,2,0:T(8,128)S(1)} %collective-permute-done.5) | data formatting | bytes 65536 | tf_op jit(solution)/shard_map/ppermute | solution.py:15
  68.7 3.7 %collective-permute-start.7 = (f32[8,8,34,1]{2,1,3,0:T(8,128)S(1)}, f32[8,8,34,1]{2,1,3,0:T(8,128)S(1)}, u32[]{:S(2)}, u32[]{:S(2)}) collective-permute-start(f32[8,8,34,1]{2,1,3,0:T(8,128)S(1)} %get-tuple-element.15), channel_id=1, source_target_pairs={{1,0},{2,1},{3,2},{0,3},{5,4},{6,5},{7,6},{4,7},{9,8},{10,9},{11,1... | collective-permute-start | bytes 26120 | tf_op jit(solution)/shard_map/ppermute | solution.py:15
  74.3 5.8 %maximum_select_fusion.1 = f32[8,8,34,130]{2,1,3,0:T(8,128)S(1)} fusion(f32[8,8,34,1]{2,1,3,0:T(8,128)S(1)} %collective-permute-done.7, f32[8,8,1,128]{2,1,3,0:T(8,128)} %copy.92, f32[8,8,32,128]{2,1,3,0:T(8,128)} %copy-done.1, f32[8,8,1,128]{2,1,3,0:T(8,128)} %copy.91, f32[8,8,34,1]{2,1,3,0:T(8,128)S(1)} %collective-permute-done.6, ...), kind=kLoop, calls=%fused_computation.2 | loop fusion | flops 1414400 | bytes 2263074 | tf_op jit(solution)/shard_map/jit(_where)/select_n | solution.py:47
  80.2 2.2 %slice_subtract_fusion.9 = (f32[8,7,32,128]{2,1,3,0:T(8,128)S(1)}, f32[8,7,32,128]{2,1,3,0:T(8,128)S(1)}) fusion(f32[8,8,34,130]{2,1,3,0:T(8,128)S(1)} %maximum_select_fusion.1), kind=kLoop, calls=%fused_computation.35 | loop fusion | flops 458752 | bytes 3670016 | tf_op jit(solution)/shard_map/sub | solution.py:27
  82.5 6.0 %fusion.27 = (f32[8,8,32]{2,1,0:T(8,128)S(1)}, f32[8,8,32,128]{2,1,3,0:T(8,128)}) fusion(f32[8,7,32,128]{2,1,3,0:T(8,128)S(1)} %get-tuple-element.19, f32[8,32,128]{1,0,2:T(8,128)S(1)} %copy-done.7, f32[8,7,32,128]{2,1,3,0:T(8,128)S(1)} %get-tuple-element.18, f32[8,32,128]{1,0,2:T(8,128)S(1)} %copy-done.6, f32[8,8,34,130]{2,1,3,0:T(8,128)S(1)} %maximum_select_fusion.1, ...), kind=kLoop, calls=%fused_computation.65 | loop fusion | flops 4454400 | bytes 8921088 | tf_op jit(solution)/shard_map/reduce_sum | solution.py:76
  88.4 19.5 %psum.14 = f32[8,8,32]{2,1,0:T(8,128)S(1)} all-reduce(f32[8,8,32]{2,1,0:T(8,128)S(1)} %get-tuple-element.12), channel_id=1, replica_groups=mesh['lat'=8,'lon'=4] {'lon'}, use_global_device_ids=true, to_apply=%region_1.2 | all-reduce | flops 2048 | bytes 16384 | tf_op jit(solution)/shard_map/psum | solution.py:76
  108.0 2.6 %multiply_add_fusion = f32[8,8,32,128]{2,1,3,0:T(8,128)S(1)} fusion(f32[8,8,32,128]{2,1,3,0:T(8,128)} %get-tuple-element.13, f32[8,8,32]{2,1,0:T(8,128)S(1)} %broadcast_multiply_fusion, f32[32]{0:T(128)S(1)} %convert_multiply_fusion), kind=kLoop, calls=%fused_computation.32 | loop fusion | flops 786432 | bytes 2105472 | tf_op jit(solution)/shard_map/add | solution.py:79
  112.6 3.7 %copy.96 = f32[8,8,32,128]{3,2,1,0:T(8,128)} copy(f32[8,8,32,128]{2,1,3,0:T(8,128)} %copy-done.2) | data formatting | bytes 2097152
  120.1 49.0 %psum.15 = bf16[2048,8]{1,0:T(8,128)(2,1)S(1)} all-reduce(f32[2048,8]{1,0:T(8,128)S(1)} %scatter_custom_fusion), channel_id=1, replica_groups=mesh['lat'=8,'lon'=4] {'lat','lon'}, use_global_device_ids=true, to_apply=%region_3.4 | all-reduce | flops 16384 | bytes 98304 | tf_op jit(solution)/shard_map/psum | solution.py:94
  169.7 2.7 %convolution_add_fusion = f32[64,416]{1,0:T(8,128)} fusion(bf16[64,2048]{1,0:T(8,128)(2,1)S(1)} %copy-done, bf16[2048,416]{1,0:T(8,128)(2,1)} %all-gather.2.cloned.1.call-done, f32[64,416]{1,0:T(8,128)S(1)} %copy.95, f32[416]{0:T(512)S(1)} %mul.174), kind=kOutput, calls=%fused_computation.39 | convolution fusion | flops 109105152 | bytes 2180736 | tf_op jit(solution)/shard_map/dot_general | solution.py:67
  (59 shorter events, 20.0 us)
Async XLA Ops:
  7.2 162.0 %copy-start = (bf16[64,2048]{1,0:T(8,128)(2,1)S(1)}, bf16[64,2048]{1,0:T(8,128)(2,1)}, u32[]{:S(2)}) copy-start(bf16[64,2048]{1,0:T(8,128)(2,1)} %param.17) | copy-start | bytes 786436
  7.2 162.5 %all-gather.2.cloned.1.call-start = ((), (), s32[]{:S(2)}) async-start(), calls=%async_computation | async-start | bytes 2162688 | tf_op jit(solution)/shard_map/all_gather | solution.py:69
  8.3 9.1 %collective-permute-start = (f32[8,8,1,128]{3,1,2,0:T(8,128)S(1)}, f32[8,8,1,128]{3,1,2,0:T(8,128)S(1)}, u32[]{:S(2)}, u32[]{:S(2)}) collective-permute-start(f32[8,8,1,128]{3,1,2,0:T(8,128)S(1)} %bitcast.37), channel_id=1, source_target_pairs={{0,4},{4,8},{8,12},{12,16},{16,20},{20,24},{24,28},{28,0},{1,5},{5... | collective-permute-start | bytes 98312 | tf_op jit(solution)/shard_map/ppermute | solution.py:14
  8.9 11.2 %collective-permute-start.1 = (f32[8,8,1,128]{3,1,2,0:T(8,128)S(1)}, f32[8,8,1,128]{3,1,2,0:T(8,128)S(1)}, u32[]{:S(2)}, u32[]{:S(2)}) collective-permute-start(f32[8,8,1,128]{3,1,2,0:T(8,128)S(1)} %bitcast.36), channel_id=1, source_target_pairs={{4,0},{8,4},{12,8},{16,12},{20,16},{24,20},{28,24},{0,28},{5,1},{9... | collective-permute-start | bytes 98312 | tf_op jit(solution)/shard_map/ppermute | solution.py:15
  23.6 9.7 %collective-permute-start.2 = (f32[8,8,34,1]{2,1,3,0:T(8,128)S(1)}, f32[8,8,34,1]{2,1,3,0:T(8,128)S(1)}, u32[]{:S(2)}, u32[]{:S(2)}) collective-permute-start(f32[8,8,34,1]{2,1,3,0:T(8,128)S(1)} %get-tuple-element.16), channel_id=1, source_target_pairs={{0,1},{1,2},{2,3},{3,0},{4,5},{5,6},{6,7},{7,4},{8,9},{9,10},{10,1... | collective-permute-start | bytes 26120 | tf_op jit(solution)/shard_map/ppermute | solution.py:14
  26.0 7.4 %collective-permute-start.3 = (f32[8,8,34,1]{2,1,3,0:T(8,128)S(1)}, f32[8,8,34,1]{2,1,3,0:T(8,128)S(1)}, u32[]{:S(2)}, u32[]{:S(2)}) collective-permute-start(f32[8,8,34,1]{2,1,3,0:T(8,128)S(1)} %get-tuple-element.17), channel_id=1, source_target_pairs={{1,0},{2,1},{3,2},{0,3},{5,4},{6,5},{7,6},{4,7},{9,8},{10,9},{11,1... | collective-permute-start | bytes 26120 | tf_op jit(solution)/shard_map/ppermute | solution.py:15
  47.6 4.6 %copy-start.1 = (f32[8,8,32,128]{2,1,3,0:T(8,128)}, f32[8,8,32,128]{2,1,3,0:T(8,128)S(1)}, u32[]{:S(2)}) copy-start(f32[8,8,32,128]{2,1,3,0:T(8,128)S(1)} %fusion.13) | copy-start | bytes 3145732
  55.1 7.1 %collective-permute-start.4 = (f32[8,8,1,128]{3,1,2,0:T(8,128)S(1)}, f32[8,8,1,128]{3,1,2,0:T(8,128)S(1)}, u32[]{:S(2)}, u32[]{:S(2)}) collective-permute-start(f32[8,8,1,128]{3,1,2,0:T(8,128)S(1)} %copy.89), channel_id=1, source_target_pairs={{0,4},{4,8},{8,12},{12,16},{16,20},{20,24},{24,28},{28,0},{1,5},{5... | collective-permute-start | bytes 98312 | tf_op jit(solution)/shard_map/ppermute | solution.py:14
  58.0 6.9 %collective-permute-start.5 = (f32[8,8,1,128]{3,1,2,0:T(8,128)S(1)}, f32[8,8,1,128]{3,1,2,0:T(8,128)S(1)}, u32[]{:S(2)}, u32[]{:S(2)}) collective-permute-start(f32[8,8,1,128]{3,1,2,0:T(8,128)S(1)} %copy.90), channel_id=1, source_target_pairs={{4,0},{8,4},{12,8},{16,12},{20,16},{24,20},{28,24},{0,28},{5,1},{9... | collective-permute-start | bytes 98312 | tf_op jit(solution)/shard_map/ppermute | solution.py:15
  68.5 5.8 %collective-permute-start.6 = (f32[8,8,34,1]{2,1,3,0:T(8,128)S(1)}, f32[8,8,34,1]{2,1,3,0:T(8,128)S(1)}, u32[]{:S(2)}, u32[]{:S(2)}) collective-permute-start(f32[8,8,34,1]{2,1,3,0:T(8,128)S(1)} %get-tuple-element.14), channel_id=1, source_target_pairs={{0,1},{1,2},{2,3},{3,0},{4,5},{5,6},{6,7},{7,4},{8,9},{9,10},{10,1... | collective-permute-start | bytes 26120 | tf_op jit(solution)/shard_map/ppermute | solution.py:14
  68.7 5.6 %collective-permute-start.7 = (f32[8,8,34,1]{2,1,3,0:T(8,128)S(1)}, f32[8,8,34,1]{2,1,3,0:T(8,128)S(1)}, u32[]{:S(2)}, u32[]{:S(2)}) collective-permute-start(f32[8,8,34,1]{2,1,3,0:T(8,128)S(1)} %get-tuple-element.15), channel_id=1, source_target_pairs={{1,0},{2,1},{3,2},{0,3},{5,4},{6,5},{7,6},{4,7},{9,8},{10,9},{11,1... | collective-permute-start | bytes 26120 | tf_op jit(solution)/shard_map/ppermute | solution.py:15
  80.1 2.3 %copy-start.3 = (f32[8,32,128]{1,0,2:T(8,128)S(1)}, f32[8,32,128]{1,0,2:T(8,128)}, u32[]{:S(2)}) copy-start(f32[8,32,128]{1,0,2:T(8,128)} %copy.84) | copy-start | bytes 393220
  80.2 2.3 %copy-start.4 = (f32[8,32,128]{1,0,2:T(8,128)S(1)}, f32[8,32,128]{1,0,2:T(8,128)}, u32[]{:S(2)}) copy-start(f32[8,32,128]{1,0,2:T(8,128)} %copy.85) | copy-start | bytes 393220
  80.2 2.3 %copy-start.5 = (f32[8,32,128]{1,0,2:T(8,128)S(1)}, f32[8,32,128]{1,0,2:T(8,128)}, u32[]{:S(2)}) copy-start(f32[8,32,128]{1,0,2:T(8,128)} %copy.86) | copy-start | bytes 393220
  80.2 2.3 %copy-start.6 = (f32[8,32,128]{1,0,2:T(8,128)S(1)}, f32[8,32,128]{1,0,2:T(8,128)}, u32[]{:S(2)}) copy-start(f32[8,32,128]{1,0,2:T(8,128)} %copy.87) | copy-start | bytes 393220
  80.2 2.3 %copy-start.7 = (f32[8,32,128]{1,0,2:T(8,128)S(1)}, f32[8,32,128]{1,0,2:T(8,128)}, u32[]{:S(2)}) copy-start(f32[8,32,128]{1,0,2:T(8,128)} %copy.88) | copy-start | bytes 393220
  110.6 2.0 %copy-start.2 = (f32[8,8,32,128]{2,1,3,0:T(8,128)}, f32[8,8,32,128]{2,1,3,0:T(8,128)S(1)}, u32[]{:S(2)}) copy-start(f32[8,8,32,128]{2,1,3,0:T(8,128)S(1)} %multiply_add_fusion) | copy-start | bytes 3145732
  112.6 3.9 %copy-start.8 = (s32[32,128]{1,0:T(8,128)S(1)}, s32[32,128]{1,0:T(8,128)}, u32[]{:S(2)}) copy-start(s32[32,128]{1,0:T(8,128)} %param.12) | copy-start | bytes 49156
  112.6 3.9 %copy-start.9 = (f32[32,128]{1,0:T(8,128)S(1)}, f32[32,128]{1,0:T(8,128)}, u32[]{:S(2)}) copy-start(f32[32,128]{1,0:T(8,128)} %param.11) | copy-start | bytes 49156
  112.6 3.7 %slice-start = ((f32[8,8,32,128]{2,1,3,0:T(8,128)}), f32[8,1,32,128]{2,1,3,0:T(1,128)S(1)}, s32[]{:S(2)}) async-start(f32[8,8,32,128]{2,1,3,0:T(8,128)} %copy-done.2), calls=%async_computation.1 | async-start | bytes 1048576 | tf_op jit(solution)/shard_map/slice | solution.py:80
Sparse Core Ops, SparseCore 0:
  12.0 58.4 all-gather.1
where the time goes:
time: 180 us; the launch traced here: 179 us
  blocking collectives  68.5 us (38%)
  local copies, waits for them, and re-layouts  38.5 us (21%)
  other arithmetic  35.8 us (20%)
  between operations  15 us (8%)
  starting transfers between devices  14.7 us (8%)
  matrix products  4.95 us (3%)
    psum x1, blocking collectives, shards(): fresh_all = lax.psum(dense, ('lat', 'lon')).astype(jnp.bfloat16)  49 us
    psum x1, blocking collectives, shards(): row_sums = lax.psum(jnp.sum(field, axis=3), 'lon')  19.5 us
    select_n x2, other arithmetic, pole_mask(): return jnp.where(outside[None, None, :, None], 0.0, padded)  11.7 us
    ppermute x4, starting transfers between devices, extended(): after = lax.ppermute(leading, axis, down)  11.6 us
    unnamed x22, local copies, waits for them, and re-layouts  9.28 us
    slice x3, local copies, waits for them, and re-layouts, extended(): last = lax.slice_in_dim(x, length - width, length, axis=dim)  8.58 us
    add x1, other arithmetic, advance(): centre + rates[0] * to_east + rates[1] * to_west + rates[2] * to_north  6.13 us
    reduce_sum x1, other arithmetic, shards(): row_sums = lax.psum(jnp.sum(field, axis=3), 'lon')  5.98 us
  transfers between devices with their start and end apart: 9, of which 1 were waited for; matrix products, arithmetic and copies ran while one was open for 41% of the time, Pallas kernels for 0%

commit v1 on v0

--- a/solution.py
+++ b/solution.py
@@ -2,6 +2,11 @@
 import jax.numpy as jnp
 from jax import lax
 from jax.sharding import PartitionSpec as P
+
+
+def axis_by_axis(array, axis_one, axis_two):
+    partial = lax.psum(array, axis_one)
+    return lax.psum(partial, axis_two)
 
 
 def extended(x, sides, width):
@@ -91,7 +96,7 @@
     )
     my_regions = lax.dynamic_index_in_dim(tile_regions, my_tile, 0, keepdims=False)
     dense = jnp.zeros((region_count, tracers), jnp.float32).at[my_regions].add(local_sums)
-    fresh_all = lax.psum(dense, ("lat", "lon")).astype(jnp.bfloat16)
+    fresh_all = axis_by_axis(dense, "lat", "lon").astype(jnp.bfloat16)
     added = jnp.dot(covariance, fresh_all, preferred_element_type=jnp.float32)
     week_hot = (jnp.arange(week_cols, dtype=jnp.int32) == week_index[0]).astype(jnp.float32)
     precond = (

time: 180 us -> 224 us (1.24)
  waiting for transfers between devices: 1.77 us -> 53 us
  blocking collectives: 68.5 us -> 63.4 us
  other arithmetic: 35.8 us -> 32.6 us
    psum x0 -> x1, waiting for transfers between devices: none -> 51.2 us  [axis_by_axis(): partial = lax.psum(array, axis_one)]
    psum x1, blocking collectives: 49 us -> 43.9 us  [axis_by_axis(): return lax.psum(partial, axis_two)]
    select_n x2, other arithmetic: 11.7 us -> 8.19 us  [pole_mask(): return jnp.where(outside[None, None, :, None], 0.0, padded)]
    unnamed x22 -> x30, local copies, waits for them, and re-layouts: 9.28 us -> 9.44 us
  transfers between devices with their start and end apart: 9 -> 10, of which waited for: 1 -> 2; matrix products, arithmetic and copies ran while one was open for 41% -> 10% of each run, Pallas kernels for 0% -> 0%
where the time goes in v1:
time: 224 us
  blocking collectives  63.4 us (28%)
  waiting for transfers between devices  53 us (24%)
  local copies, waits for them, and re-layouts  38.9 us (17%)
  other arithmetic  32.6 us (15%)
  between operations  16.5 us (7%)
  starting transfers between devices  14.7 us (7%)
  matrix products  4.95 us (2%)
    psum x1, waiting for transfers between devices, axis_by_axis(): partial = lax.psum(array, axis_one)  51.2 us
    psum x1, blocking collectives, axis_by_axis(): return lax.psum(partial, axis_two)  43.9 us
    psum x1, blocking collectives, shards(): row_sums = lax.psum(jnp.sum(field, axis=3), 'lon')  19.5 us
    ppermute x4, starting transfers between devices, extended(): after = lax.ppermute(leading, axis, down)  11.7 us
    unnamed x30, local copies, waits for them, and re-layouts  9.44 us
    slice x3, local copies, waits for them, and re-layouts, extended(): last = lax.slice_in_dim(x, length - width, length, axis=dim)  8.59 us
    select_n x2, other arithmetic, pole_mask(): return jnp.where(outside[None, None, :, None], 0.0, padded)  8.19 us
    add x1, other arithmetic, advance(): centre + rates[0] * to_east + rates[1] * to_west + rates[2] * to_north  6.13 us
  transfers between devices with their start and end apart: 10, of which 2 were waited for; matrix products, arithmetic and copies ran while one was open for 10% of the time, Pallas kernels for 0%

profile of v1, /device:TPU:0, one launch (start us, length us, event | category | flops | bytes accessed | tf_op | source)
XLA Modules:
  0.0 224.0 jit_solution(10577379408875572229)
XLA Ops:
  9.7 2.9 %collective-permute-start.1 = (f32[8,8,1,128]{3,1,2,0:T(8,128)S(1)}, f32[8,8,1,128]{3,1,2,0:T(8,128)S(1)}, u32[]{:S(2)}, u32[]{:S(2)}) collective-permute-start(f32[8,8,1,128]{3,1,2,0:T(8,128)S(1)} %bitcast.36), channel_id=1, source_target_pairs={{4,0},{8,4},{12,8},{16,12},{20,16},{24,20},{28,24},{0,28},{5,1},{9... | collective-permute-start | bytes 98312 | tf_op jit(solution)/shard_map/ppermute | solution.py:20
  13.9 3.7 %copy.81 = f32[8,8,32,128]{2,1,3,0:T(8,128)} copy(f32[8,8,32,128]{3,2,1,0:T(8,128)} %param.9) | data formatting | bytes 2097152 | tf_op args[0]
  17.6 2.6 %copy.80 = f32[8,8,1,128]{2,1,3,0:T(8,128)} copy(f32[8,8,1,128]{3,1,2,0:T(8,128)S(1)} %collective-permute-done) | data formatting | bytes 65536 | tf_op jit(solution)/shard_map/ppermute | solution.py:19
  20.2 2.6 %copy.82 = f32[8,8,1,128]{2,1,3,0:T(8,128)} copy(f32[8,8,1,128]{3,1,2,0:T(8,128)S(1)} %collective-permute-done.1) | data formatting | bytes 65536 | tf_op jit(solution)/shard_map/ppermute | solution.py:20
  23.8 2.3 %collective-permute-start.2 = (f32[8,8,34,1]{2,1,3,0:T(8,128)S(1)}, f32[8,8,34,1]{2,1,3,0:T(8,128)S(1)}, u32[]{:S(2)}, u32[]{:S(2)}) collective-permute-start(f32[8,8,34,1]{2,1,3,0:T(8,128)S(1)} %get-tuple-element.16), channel_id=1, source_target_pairs={{0,1},{1,2},{2,3},{3,0},{4,5},{5,6},{6,7},{7,4},{8,9},{9,10},{10,1... | collective-permute-start | bytes 26120 | tf_op jit(solution)/shard_map/ppermute | solution.py:19
  33.5 5.8 %maximum_select_fusion = f32[8,8,34,130]{2,1,3,0:T(8,128)S(1)} fusion(f32[8,8,34,1]{2,1,3,0:T(8,128)S(1)} %collective-permute-done.3, f32[8,8,1,128]{2,1,3,0:T(8,128)} %copy.82, f32[8,8,32,128]{2,1,3,0:T(8,128)} %copy.81, f32[8,8,1,128]{2,1,3,0:T(8,128)} %copy.80, f32[8,8,34,1]{2,1,3,0:T(8,128)S(1)} %collective-permute-done.2, pred[34]{0:T(512)(128)(4,1)S(1)} %and_or_fusion), kind=kLoop, calls=%fused_computation.1 | loop fusion | flops 1414400 | bytes 2263074 | tf_op jit(solution)/shard_map/jit(_where)/select_n | solution.py:52
  39.4 2.2 slice_subtract_fusion.11
  41.6 6.1 %fusion.13 = f32[8,8,32,128]{2,1,3,0:T(8,128)S(1)} fusion(f32[8,8,34,130]{2,1,3,0:T(8,128)S(1)} %maximum_select_fusion, f32[8,7,32,128]{2,1,3,0:T(8,128)S(1)} %get-tuple-element.21, f32[8,7,32,128]{2,1,3,0:T(8,128)S(1)} %get-tuple-element.20, f32[8,32,128]{1,0,2:T(8,128)} %copy.88, f32[8,32,128]{1,0,2:T(8,128)} %copy.87, f32[8,32,128]{1,0,2:T(8,128)} %copy.86, ...), kind=kLoop, calls=%fused_computation.21 | loop fusion | flops 4194304 | bytes 8912896 | tf_op jit(solution)/shard_map/add | solution.py:35
  47.7 4.6 %fusion.29 = (f32[8,8,1,128]{2,1,3,0:T(8,128)}, f32[8,8,1,128]{2,1,3,0:T(8,128)}) fusion(f32[8,8,32,128]{2,1,3,0:T(8,128)S(1)} %fusion.13), kind=kLoop, calls=%fused_computation.66 | loop fusion | bytes 131072 | tf_op jit(solution)/shard_map/slice | solution.py:17
  52.4 2.9 %copy.89 = f32[8,8,1,128]{3,1,2,0:T(8,128)S(1)} copy(f32[8,8,1,128]{2,1,3,0:T(8,128)} %get-tuple-element.22) | data formatting | bytes 65536 | tf_op jit(solution)/shard_map/slice | solution.py:17
  55.3 2.9 %copy.90 = f32[8,8,1,128]{3,1,2,0:T(8,128)S(1)} copy(f32[8,8,1,128]{2,1,3,0:T(8,128)} %get-tuple-element.23) | data formatting | bytes 65536 | tf_op jit(solution)/shard_map/slice | solution.py:18
  58.1 2.9 %collective-permute-start.5 = (f32[8,8,1,128]{3,1,2,0:T(8,128)S(1)}, f32[8,8,1,128]{3,1,2,0:T(8,128)S(1)}, u32[]{:S(2)}, u32[]{:S(2)}) collective-permute-start(f32[8,8,1,128]{3,1,2,0:T(8,128)S(1)} %copy.90), channel_id=1, source_target_pairs={{4,0},{8,4},{12,8},{16,12},{20,16},{24,20},{28,24},{0,28},{5,1},{9... | collective-permute-start | bytes 98312 | tf_op jit(solution)/shard_map/ppermute | solution.py:20
  61.0 2.7 %copy.91 = f32[8,8,1,128]{2,1,3,0:T(8,128)} copy(f32[8,8,1,128]{3,1,2,0:T(8,128)S(1)} %collective-permute-done.4) | data formatting | bytes 65536 | tf_op jit(solution)/shard_map/ppermute | solution.py:19
  63.7 2.7 %copy.92 = f32[8,8,1,128]{2,1,3,0:T(8,128)} copy(f32[8,8,1,128]{3,1,2,0:T(8,128)S(1)} %collective-permute-done.5) | data formatting | bytes 65536 | tf_op jit(solution)/shard_map/ppermute | solution.py:20
  67.5 3.8 %collective-permute-start.7 = (f32[8,8,34,1]{2,1,3,0:T(8,128)S(1)}, f32[8,8,34,1]{2,1,3,0:T(8,128)S(1)}, u32[]{:S(2)}, u32[]{:S(2)}) collective-permute-start(f32[8,8,34,1]{2,1,3,0:T(8,128)S(1)} %get-tuple-element.15), channel_id=1, source_target_pairs={{1,0},{2,1},{3,2},{0,3},{5,4},{6,5},{7,6},{4,7},{9,8},{10,9},{11,1... | collective-permute-start | bytes 26120 | tf_op jit(solution)/shard_map/ppermute | solution.py:20
  73.2 2.3 %maximum_select_fusion.1 = f32[8,8,34,130]{2,1,3,0:T(8,128)S(1)} fusion(f32[8,8,34,1]{2,1,3,0:T(8,128)S(1)} %collective-permute-done.7, f32[8,8,1,128]{2,1,3,0:T(8,128)S(1)} %copy-done.4, f32[8,8,32,128]{2,1,3,0:T(8,128)S(1)} %copy-done.2, f32[8,8,1,128]{2,1,3,0:T(8,128)S(1)} %copy-done.3, f32[8,8,34,1]{2,1,3,0:T(8,128)S(1)} %collective-permute-done.6, ...), kind=kLoop, calls=%fused_computation.2 | loop fusion | flops 1414400 | bytes 2263074 | tf_op jit(solution)/shard_map/jit(_where)/select_n | solution.py:52
  77.9 6.0 %fusion.27 = (f32[8,8,32]{2,1,0:T(8,128)S(1)}, f32[8,8,32,128]{2,1,3,0:T(8,128)}) fusion(f32[8,7,32,128]{2,1,3,0:T(8,128)S(1)} %get-tuple-element.19, f32[8,32,128]{1,0,2:T(8,128)S(1)} %copy-done.10, f32[8,7,32,128]{2,1,3,0:T(8,128)S(1)} %get-tuple-element.18, f32[8,32,128]{1,0,2:T(8,128)S(1)} %copy-done.9, f32[8,8,34,130]{2,1,3,0:T(8,128)S(1)} %maximum_select_fusion.1, ...), kind=kLoop, calls=%fused_computation.65 | loop fusion | flops 4454400 | bytes 8921088 | tf_op jit(solution)/shard_map/reduce_sum | solution.py:81
  83.9 19.5 %psum.21 = f32[8,8,32]{2,1,0:T(8,128)S(1)} all-reduce(f32[8,8,32]{2,1,0:T(8,128)S(1)} %get-tuple-element.12), channel_id=1, replica_groups=mesh['lat'=8,'lon'=4] {'lon'}, use_global_device_ids=true, to_apply=%region_1.2 | all-reduce | flops 2048 | bytes 16384 | tf_op jit(solution)/shard_map/psum | solution.py:81
  103.4 2.6 %multiply_add_fusion = f32[8,8,32,128]{2,1,3,0:T(8,128)S(1)} fusion(f32[8,8,32,128]{2,1,3,0:T(8,128)} %get-tuple-element.13, f32[8,8,32]{2,1,0:T(8,128)S(1)} %broadcast_multiply_fusion, f32[32]{0:T(128)S(1)} %convert_multiply_fusion), kind=kLoop, calls=%fused_computation.32 | loop fusion | flops 786432 | bytes 2105472 | tf_op jit(solution)/shard_map/add | solution.py:84
  110.5 2.5 %scatter_custom_fusion = f32[2048,8]{1,0:T(8,128)} fusion(s32[256]{0:T(256)S(1)} %bitcast.38, f32[256,8]{1,0:T(8,128)S(1)} %fusion.20, f32[]{:T(128)} %constant.8.clone.1), kind=kCustom, calls=%fused_computation.42 | custom fusion | flops 2048 | bytes 65540 | tf_op jit(solution)/shard_map/scatter-add | solution.py:98
  114.4 3.8 %copy.96 = f32[8,8,32,128]{3,2,1,0:T(8,128)} copy(f32[8,8,32,128]{2,1,3,0:T(8,128)} %copy-done.5) | data formatting | bytes 2097152
  118.2 51.2 %all-reduce.6.cloned.1.call-done = f32[2048,8]{1,0:T(8,128)} async-done(((f32[2048,8]{1,0:T(8,128)}), f32[2048,8]{1,0:T(8,128)}) %all-reduce.6.cloned.1.call-update) | async-done | bytes 65552 | tf_op jit(solution)/shard_map/psum | solution.py:8
  169.4 43.9 %psum.23 = bf16[2048,8]{1,0:T(8,128)(2,1)S(1)} all-reduce(f32[2048,8]{1,0:T(8,128)} %all-reduce.6.cloned.1.call-done), channel_id=1, replica_groups=mesh['lat'=8,'lon'=4] {'lon'}, use_global_device_ids=true, to_apply=%region_4.5 | all-reduce | flops 16384 | bytes 98304 | tf_op jit(solution)/shard_map/psum | solution.py:9
  213.8 2.7 %convolution_add_fusion = f32[64,416]{1,0:T(8,128)} fusion(bf16[64,2048]{1,0:T(8,128)(2,1)S(1)} %copy-done, bf16[2048,416]{1,0:T(8,128)(2,1)} %all-gather.2.cloned.1.call-done, f32[64,416]{1,0:T(8,128)S(1)} %copy.95, f32[416]{0:T(512)S(1)} %mul.174), kind=kOutput, calls=%fused_computation.39 | convolution fusion | flops 109105152 | bytes 2180736 | tf_op jit(solution)/shard_map/dot_general | solution.py:72
  (69 shorter events, 22.3 us)
Async XLA Ops:
  8.0 205.3 %copy-start = (bf16[64,2048]{1,0:T(8,128)(2,1)S(1)}, bf16[64,2048]{1,0:T(8,128)(2,1)}, u32[]{:S(2)}) copy-start(bf16[64,2048]{1,0:T(8,128)(2,1)} %param.17) | copy-start | bytes 786436
  8.0 161.4 %all-reduce.6.cloned.1.call-start = ((), (), s32[]{:S(2)}) async-start(), calls=%async_computation.1 | async-start | bytes 2097152 | tf_op jit(solution)/shard_map/psum | solution.py:8
  9.2 8.4 %collective-permute-start = (f32[8,8,1,128]{3,1,2,0:T(8,128)S(1)}, f32[8,8,1,128]{3,1,2,0:T(8,128)S(1)}, u32[]{:S(2)}, u32[]{:S(2)}) collective-permute-start(f32[8,8,1,128]{3,1,2,0:T(8,128)S(1)} %bitcast.37), channel_id=1, source_target_pairs={{0,4},{4,8},{8,12},{12,16},{16,20},{20,24},{24,28},{28,0},{1,5},{5... | collective-permute-start | bytes 98312 | tf_op jit(solution)/shard_map/ppermute | solution.py:19
  9.7 10.5 %collective-permute-start.1 = (f32[8,8,1,128]{3,1,2,0:T(8,128)S(1)}, f32[8,8,1,128]{3,1,2,0:T(8,128)S(1)}, u32[]{:S(2)}, u32[]{:S(2)}) collective-permute-start(f32[8,8,1,128]{3,1,2,0:T(8,128)S(1)} %bitcast.36), channel_id=1, source_target_pairs={{4,0},{8,4},{12,8},{16,12},{20,16},{24,20},{28,24},{0,28},{5,1},{9... | collective-permute-start | bytes 98312 | tf_op jit(solution)/shard_map/ppermute | solution.py:20
  23.8 9.8 %collective-permute-start.2 = (f32[8,8,34,1]{2,1,3,0:T(8,128)S(1)}, f32[8,8,34,1]{2,1,3,0:T(8,128)S(1)}, u32[]{:S(2)}, u32[]{:S(2)}) collective-permute-start(f32[8,8,34,1]{2,1,3,0:T(8,128)S(1)} %get-tuple-element.16), channel_id=1, source_target_pairs={{0,1},{1,2},{2,3},{3,0},{4,5},{5,6},{6,7},{7,4},{8,9},{9,10},{10,1... | collective-permute-start | bytes 26120 | tf_op jit(solution)/shard_map/ppermute | solution.py:19
  26.1 7.4 %collective-permute-start.3 = (f32[8,8,34,1]{2,1,3,0:T(8,128)S(1)}, f32[8,8,34,1]{2,1,3,0:T(8,128)S(1)}, u32[]{:S(2)}, u32[]{:S(2)}) collective-permute-start(f32[8,8,34,1]{2,1,3,0:T(8,128)S(1)} %get-tuple-element.17), channel_id=1, source_target_pairs={{1,0},{2,1},{3,2},{0,3},{5,4},{6,5},{7,6},{4,7},{9,8},{10,9},{11,1... | collective-permute-start | bytes 26120 | tf_op jit(solution)/shard_map/ppermute | solution.py:20
  47.7 4.6 %copy-start.1 = (f32[8,8,32,128]{2,1,3,0:T(8,128)}, f32[8,8,32,128]{2,1,3,0:T(8,128)S(1)}, u32[]{:S(2)}) copy-start(f32[8,8,32,128]{2,1,3,0:T(8,128)S(1)} %fusion.13) | copy-start | bytes 3145732
  52.4 8.6 %copy-start.13 = (s32[32]{0:T(128)S(1)}, s32[32]{0:T(128)}, u32[]{:S(2)}) copy-start(s32[32]{0:T(128)} %param.14) | copy-start | bytes 388
  55.2 5.8 %collective-permute-start.4 = (f32[8,8,1,128]{3,1,2,0:T(8,128)S(1)}, f32[8,8,1,128]{3,1,2,0:T(8,128)S(1)}, u32[]{:S(2)}, u32[]{:S(2)}) collective-permute-start(f32[8,8,1,128]{3,1,2,0:T(8,128)S(1)} %copy.89), channel_id=1, source_target_pairs={{0,4},{4,8},{8,12},{12,16},{16,20},{20,24},{24,28},{28,0},{1,5},{5... | collective-permute-start | bytes 98312 | tf_op jit(solution)/shard_map/ppermute | solution.py:19
  58.1 5.5 %collective-permute-start.5 = (f32[8,8,1,128]{3,1,2,0:T(8,128)S(1)}, f32[8,8,1,128]{3,1,2,0:T(8,128)S(1)}, u32[]{:S(2)}, u32[]{:S(2)}) collective-permute-start(f32[8,8,1,128]{3,1,2,0:T(8,128)S(1)} %copy.90), channel_id=1, source_target_pairs={{4,0},{8,4},{12,8},{16,12},{20,16},{24,20},{28,24},{0,28},{5,1},{9... | collective-permute-start | bytes 98312 | tf_op jit(solution)/shard_map/ppermute | solution.py:20
  66.3 6.9 %copy-start.2 = (f32[8,8,32,128]{2,1,3,0:T(8,128)S(1)}, f32[8,8,32,128]{2,1,3,0:T(8,128)}, u32[]{:S(2)}) copy-start(f32[8,8,32,128]{2,1,3,0:T(8,128)} %copy-done.1) | copy-start | bytes 3145732
  66.3 6.9 %copy-start.3 = (f32[8,8,1,128]{2,1,3,0:T(8,128)S(1)}, f32[8,8,1,128]{2,1,3,0:T(8,128)}, u32[]{:S(2)}) copy-start(f32[8,8,1,128]{2,1,3,0:T(8,128)} %copy.91) | copy-start | bytes 98308
  66.3 6.9 %copy-start.4 = (f32[8,8,1,128]{2,1,3,0:T(8,128)S(1)}, f32[8,8,1,128]{2,1,3,0:T(8,128)}, u32[]{:S(2)}) copy-start(f32[8,8,1,128]{2,1,3,0:T(8,128)} %copy.92) | copy-start | bytes 98308
  67.4 5.8 %collective-permute-start.6 = (f32[8,8,34,1]{2,1,3,0:T(8,128)S(1)}, f32[8,8,34,1]{2,1,3,0:T(8,128)S(1)}, u32[]{:S(2)}, u32[]{:S(2)}) collective-permute-start(f32[8,8,34,1]{2,1,3,0:T(8,128)S(1)} %get-tuple-element.14), channel_id=1, source_target_pairs={{0,1},{1,2},{2,3},{3,0},{4,5},{5,6},{6,7},{7,4},{8,9},{9,10},{10,1... | collective-permute-start | bytes 26120 | tf_op jit(solution)/shard_map/ppermute | solution.py:19
  67.5 5.7 %collective-permute-start.7 = (f32[8,8,34,1]{2,1,3,0:T(8,128)S(1)}, f32[8,8,34,1]{2,1,3,0:T(8,128)S(1)}, u32[]{:S(2)}, u32[]{:S(2)}) collective-permute-start(f32[8,8,34,1]{2,1,3,0:T(8,128)S(1)} %get-tuple-element.15), channel_id=1, source_target_pairs={{1,0},{2,1},{3,2},{0,3},{5,4},{6,5},{7,6},{4,7},{9,8},{10,9},{11,1... | collective-permute-start | bytes 26120 | tf_op jit(solution)/shard_map/ppermute | solution.py:20
  75.6 2.3 %copy-start.6 = (f32[8,32,128]{1,0,2:T(8,128)S(1)}, f32[8,32,128]{1,0,2:T(8,128)}, u32[]{:S(2)}) copy-start(f32[8,32,128]{1,0,2:T(8,128)} %copy.84) | copy-start | bytes 393220
  75.6 2.3 %copy-start.7 = (f32[8,32,128]{1,0,2:T(8,128)S(1)}, f32[8,32,128]{1,0,2:T(8,128)}, u32[]{:S(2)}) copy-start(f32[8,32,128]{1,0,2:T(8,128)} %copy.85) | copy-start | bytes 393220
  75.6 2.3 %copy-start.8 = (f32[8,32,128]{1,0,2:T(8,128)S(1)}, f32[8,32,128]{1,0,2:T(8,128)}, u32[]{:S(2)}) copy-start(f32[8,32,128]{1,0,2:T(8,128)} %copy.86) | copy-start | bytes 393220
  75.6 2.3 %copy-start.9 = (f32[8,32,128]{1,0,2:T(8,128)S(1)}, f32[8,32,128]{1,0,2:T(8,128)}, u32[]{:S(2)}) copy-start(f32[8,32,128]{1,0,2:T(8,128)} %copy.87) | copy-start | bytes 393220
  75.6 2.3 %copy-start.10 = (f32[8,32,128]{1,0,2:T(8,128)S(1)}, f32[8,32,128]{1,0,2:T(8,128)}, u32[]{:S(2)}) copy-start(f32[8,32,128]{1,0,2:T(8,128)} %copy.88) | copy-start | bytes 393220
  103.4 5.2 %copy-start.11 = (s32[32,128]{1,0:T(8,128)S(1)}, s32[32,128]{1,0:T(8,128)}, u32[]{:S(2)}) copy-start(s32[32,128]{1,0:T(8,128)} %param.12) | copy-start | bytes 49156
  103.4 5.2 %copy-start.12 = (f32[32,128]{1,0:T(8,128)S(1)}, f32[32,128]{1,0:T(8,128)}, u32[]{:S(2)}) copy-start(f32[32,128]{1,0:T(8,128)} %param.11) | copy-start | bytes 49156
  106.0 1.9 copy-start.5
  113.0 100.7 %all-gather.2.cloned.1.call-start = ((), (), s32[]{:S(2)}) async-start(), calls=%async_computation | async-start | bytes 2162688 | tf_op jit(solution)/shard_map/all_gather | solution.py:74
Sparse Core Ops, SparseCore 0:
  113.2 56.2 all-reduce.5
Sparse Core Ops, SparseCore 1:
  116.5 53.9 all-gather.1
